TPU v7x, 128 devices: a whole 4x4x4 slice. The times are simulated.
128 devices in a mesh: tm: 64 (over x, z, y), head: 2 (over core).
Axes of the slice: x: 4, y: 4, z: 4, core: 2. Of those that a mesh axis runs over, the one named last changes fastest.
Arguments:
- series: bfloat16 [16, 65536, 512], P(None, 'tm'), may hold values from -6 to 6
- modes: int32 [128], replicated, may hold values from 1 to 32767, as said below
- query_weight: bfloat16 [512, 512], P(None, 'head'), may hold values from -0.25 to 0.25
- mix_weight: float32 [128, 8, 64, 128], P('tm', 'head'), may hold values from -0.5 to 0.5
- out_weight: bfloat16 [512, 512], P(None, 'head'), may hold values from -0.25 to 0.25
Outputs:
- output: bfloat16 [16, 65536, 512], P(None, 'tm', 'head')
Inputs may be any that keep to these rules, and one draw needn't show every extreme that they name: `modes`: distinct mode numbers; both 1 and one less than half of 65536 are among them.
All inputs are finite; a program needn't handle non-finite values.
Results may differ from a plain program's by a relative error of at most 0.0075.
Values may be sent and summed in bfloat16 or wider, within the bound.
A program may use at most 128 MiB of HBM per device.

v0:
```python
import math

import jax
import jax.numpy as jnp
from jax import lax
from jax.sharding import PartitionSpec as P

two_pi = 2.0 * math.pi


def wave_tables(mode_list, first_time, time_count, series_length):
    time_index = first_time + lax.iota(jnp.int32, time_count)
    phases = time_index[:, None] * mode_list[None, :] % series_length
    angles = phases.astype(jnp.float32) * (two_pi / series_length)
    return (jnp.cos(angles).astype(jnp.bfloat16), jnp.sin(angles).astype(jnp.bfloat16))


def body(series, modes, query_weight, mix_weight, out_weight):
    series_count, shard_rows, model_width = series.shape
    group_width = query_weight.shape[1]
    mode_total = modes.shape[0]
    own_modes = mix_weight.shape[0]
    heads_here = mix_weight.shape[1]
    head_size = mix_weight.shape[2]
    series_length = lax.axis_size("tm") * shard_rows
    first_time = lax.axis_index("tm") * shard_rows
    forward_scale = 1.0 / math.sqrt(series_length)
    inverse_scale = 1.0 / math.sqrt(mode_total)
    queries = jnp.dot(
        series.reshape(series_count * shard_rows, model_width),
        query_weight,
        preferred_element_type=jnp.float32,
    )
    queries = queries.astype(jnp.bfloat16).reshape(series_count, shard_rows, group_width)
    cosine, sine_part = wave_tables(modes, first_time, shard_rows, series_length)
    real_part = jnp.einsum("tm,btf->mbf", cosine, queries, preferred_element_type=jnp.float32)
    imag_part = jnp.einsum("tm,btf->mbf", sine_part, queries, preferred_element_type=jnp.float32)
    summed_all = lax.psum(jnp.stack([real_part, -imag_part], axis=1) * forward_scale, "tm")
    spectrum = lax.dynamic_slice_in_dim(summed_all, lax.axis_index("tm") * own_modes, own_modes, 0)
    spec_parts = spectrum.reshape(own_modes, 2, series_count, heads_here, head_size)
    from_real = jnp.einsum(
        "mbhi,mhio->mbho", spec_parts[:, 0], mix_weight, precision=lax.Precision.HIGHEST
    )
    from_imag = jnp.einsum(
        "mbhi,mhio->mbho", spec_parts[:, 1], mix_weight, precision=lax.Precision.HIGHEST
    )
    mixed_real = from_real[..., :head_size] - from_imag[..., head_size:]
    mixed_imag = from_real[..., head_size:] + from_imag[..., :head_size]
    mixed_spectra = jnp.stack([mixed_real, mixed_imag], axis=1).reshape(
        own_modes, 2, series_count, group_width
    )
    mixed_spectra = mixed_spectra.astype(jnp.bfloat16)
    cosine, sine_part = wave_tables(modes, first_time, shard_rows, series_length)
    wave_table = jnp.concatenate([cosine, -sine_part], axis=1)
    by_mode = lax.all_gather(mixed_spectra, "tm", axis=0, tiled=True)
    all_spectra = lax.all_gather(by_mode, "head", axis=3, tiled=True)
    stacked = jnp.concatenate([all_spectra[:, 0], all_spectra[:, 1]], axis=0)
    summed = jnp.einsum("tk,kbf->btf", wave_table, stacked, preferred_element_type=jnp.float32)
    restored = (summed * inverse_scale).astype(jnp.bfloat16)
    output = jnp.dot(
        restored.reshape(series_count * shard_rows, model_width),
        out_weight,
        preferred_element_type=jnp.float32,
    )
    return output.astype(jnp.bfloat16).reshape(series_count, shard_rows, group_width)


def solution(mesh):
    in_specs = (
        P(None, "tm", None),
        P(),
        P(None, "head"),
        P("tm", "head", None, None),
        P(None, "head"),
    )
    out_specs = P(None, "tm", "head")
    return jax.shard_map(body, mesh=mesh, in_specs=in_specs, out_specs=out_specs, check_vma=False)
```

profile of v0, /device:TPU:0, one launch (start us, length us, event | category | flops | bytes accessed | tf_op | source)
XLA Modules:
  0.0 305.2 jit_solution(206311727932910354)
XLA Ops:
  6.5 0.0 copy-start
  6.5 0.0 all-reduce.2.cloned.1.call-start
  6.5 0.9 copy-done
  7.5 10.3 %convolution_convert_fusion.1 = bf16[16384,256]{1,0:T(8,128)(2,1)S(1)} fusion(bf16[16384,512]{1,0:T(8,128)(2,1)} %bitcast.50, bf16[512,256]{1,0:T(8,128)(2,1)S(1)} %copy-done), kind=kOutput, calls=%fused_computation.2 | convolution fusion | flops 4299161600 | bytes 25427968 | tf_op jit(solution)/shard_map/dot_general | solution.py:29
  17.8 3.0 negate_bitcast_fusion
  20.8 3.0 convolution_bitcast_fusion
  23.8 2.4 maximum_multiply_fusion
  26.2 0.0 all-reduce.2.cloned.1.call-update
  26.2 0.0 all-gather.3.cloned.1.call-start
  26.3 141.3 %all-reduce.2.cloned.1.call-done = f32[128,2,16,256]{3,0,2,1:T(8,128)} async-done(((f32[128,2,16,256]{3,0,2,1:T(8,128)}), f32[128,2,16,256]{3,0,2,1:T(8,128)}) %all-reduce.2.cloned.1.call-update) | async-done | bytes 4194320 | tf_op jit(solution)/shard_map/psum | solution.py:38
  167.6 1.0 constant_dynamic-slice_fusion
  168.5 0.1 reshape.35
  168.7 0.3 convolution_bitcast_fusion.2
  169.0 0.3 convolution_bitcast_fusion.1
  169.4 0.1 fusion.13
  169.5 0.1 stack.21
  169.6 0.1 stack.22
  169.7 0.6 pad_maximum_fusion
  170.4 0.0 all-gather.3.cloned.1.call-update
  170.4 0.2 all-gather.5.cloned.1.call-start
  170.6 63.5 %all-gather.3.cloned.1.call-done = bf16[128,2,16,256]{3,2,1,0:T(8,128)(2,1)} async-done(((bf16[2,2,16,256]{3,2,1,0:T(8,128)(2,1)}), bf16[128,2,16,256]{3,2,1,0:T(8,128)(2,1)}) %all-gather.3.cloned.1.call-update) | async-done | bytes 2097168 | tf_op jit(solution)/shard_map/all_gather | solution.py:55
  234.1 4.5 %copy.27 = bf16[128,2,16,256]{0,3,2,1:T(8,128)(2,1)} copy(bf16[128,2,16,256]{3,2,1,0:T(8,128)(2,1)} %all-gather.3.cloned.1.call-done) | data formatting | bytes 4194304 | tf_op jit(solution)/shard_map/all_gather | solution.py:55
  238.6 0.0 all-gather.5.cloned.1.call-update
  238.6 2.3 fusion.11
  240.9 2.3 cosine_convert_fusion
  243.2 9.4 %all-gather.5.cloned.1.call-done = bf16[128,2,16,512]{0,3,2,1:T(8,128)(2,1)} async-done(((bf16[128,2,16,256]{0,3,2,1:T(8,128)(2,1)}), bf16[128,2,16,512]{0,3,2,1:T(8,128)(2,1)}) %all-gather.5.cloned.1.call-update) | async-done | bytes 4194320 | tf_op jit(solution)/shard_map/all_gather | solution.py:56
  252.6 2.5 slice_bitcast_fusion.1
  255.1 8.2 %fusion = bf16[16,1024,512]{1,2,0:T(8,128)(2,1)} fusion(bf16[128,16,512]{0,2,1:T(8,128)(2,1)S(1)} %get-tuple-element.6, bf16[128,16,512]{0,2,1:T(8,128)(2,1)S(1)} %get-tuple-element.5, bf16[1024,128]{1,0:T(8,128)(2,1)S(1)} %fusion.11, bf16[1024,128]{1,0:T(8,128)(2,1)S(1)} %cosine_convert_fusion), kind=kOutput, calls=%fused_computation.3 | convolution fusion | flops 4321181696 | bytes 21495808 | tf_op jit(solution)/shard_map/tk,kbf->btf/dot_general | solution.py:58
  263.3 21.7 %copy.28 = bf16[16,1024,512]{2,1,0:T(8,128)(2,1)} copy(bf16[16,1024,512]{1,2,0:T(8,128)(2,1)} %fusion) | data formatting | bytes 33554432 | tf_op jit(solution)/shard_map/convert_element_type | solution.py:59
  285.0 0.0 copy-done.4
  285.0 13.7 %convolution_convert_fusion = bf16[16384,256]{1,0:T(8,128)(2,1)} fusion(bf16[16384,512]{1,0:T(8,128)(2,1)} %bitcast.47, bf16[512,256]{1,0:T(8,128)(2,1)S(1)} %copy-done.4), kind=kOutput, calls=%fused_computation.1 | convolution fusion | flops 4299161600 | bytes 25427968 | tf_op jit(solution)/shard_map/dot_general | solution.py:60
  298.7 0.0 copy-done.1
  (10 shorter events, 0.1 us)
Async XLA Ops:
  6.5 1.0 copy-start
  6.5 161.0 %all-reduce.2.cloned.1.call-start = ((), (), s32[]{:S(2)}) async-start(), calls=%async_computation | async-start | bytes 8388608 | tf_op jit(solution)/shard_map/psum | solution.py:38
  7.5 10.3 %copy-start.3 = (s32[128]{0:T(128)S(1)}, s32[128]{0:T(128)}, u32[]{:S(2)}) copy-start(s32[128]{0:T(128)} %param.6) | copy-start | bytes 1540
  26.2 142.5 %copy-start.2 = (f32[2,4,64,128]{3,2,1,0:T(8,128)S(1)}, f32[2,4,64,128]{3,2,1,0:T(8,128)}, u32[]{:S(2)}) copy-start(f32[2,4,64,128]{3,2,1,0:T(8,128)} %param.8) | copy-start | bytes 786436
  26.2 207.9 %all-gather.3.cloned.1.call-start = ((), (), s32[]{:S(2)}) async-start(), calls=%async_computation.1 | async-start | bytes 2129920 | tf_op jit(solution)/shard_map/all_gather | solution.py:55
  170.4 82.2 %all-gather.5.cloned.1.call-start = ((), (), s32[]{:S(2)}) async-start(), calls=%async_computation.2 | async-start | bytes 6291456 | tf_op jit(solution)/shard_map/all_gather | solution.py:56
  263.3 21.7 %copy-start.4 = (bf16[512,256]{1,0:T(8,128)(2,1)S(1)}, bf16[512,256]{1,0:T(8,128)(2,1)}, u32[]{:S(2)}) copy-start(bf16[512,256]{1,0:T(8,128)(2,1)} %param.9) | copy-start | bytes 786436
  285.0 13.7 %copy-start.1 = (bf16[512,256]{1,0:T(8,128)(2,1)S(1)}, bf16[512,256]{1,0:T(8,128)(2,1)}, u32[]{:S(2)}) copy-start(bf16[512,256]{1,0:T(8,128)(2,1)} %param.7) | copy-start | bytes 786436
Sparse Core Ops, SparseCore 0:
  26.4 141.1 all-reduce.1
  170.8 63.2 all-gather.2
  238.8 13.8 all-gather.4
where the time goes:
time: 307 us; the launch traced here: 305 us
  waiting for transfers between devices  214 us (70%)
  matrix products  38.9 us (13%)
  local copies, waits for them, and re-layouts  31 us (10%)
  between operations  13.2 us (4%)
  other arithmetic  7.68 us (3%)
    psum x1, waiting for transfers between devices, body(): lax.psum(jnp.stack([real_part, -imag_part], axis=1) * forward_scale, 'tm')  141 us
    all_gather x1, waiting for transfers between devices, body(): by_mode = lax.all_gather(mixed_spectra, 'tm', axis=0, tiled=True)  63.5 us
    convert_element_type x1, local copies, waits for them, and re-layouts, body(): restored = (summed * inverse_scale).astype(jnp.bfloat16)  21.7 us
    dot_general x1, matrix products, body(): jnp.dot(restored.reshape(series_count * shard_rows, model_width), out_wei...  13.7 us
    dot_general x1, matrix products, body(): jnp.dot(series.reshape(series_count * shard_rows, model_width), query_wei...  10.3 us
    all_gather x1, waiting for transfers between devices, body(): all_spectra = lax.all_gather(by_mode, 'head', axis=3, tiled=True)  9.43 us
    dot_general x1, matrix products, body(): jnp.einsum('tk,kbf->btf', wave_table, stacked, preferred_element_type=jnp...  8.16 us
  transfers between devices with their start and end apart: 3, of which 3 were waited for; matrix products, arithmetic and copies ran while one was open for 1% of the time, Pallas kernels for 0%

commit v1 on v0

v1 whole, which is shorter than its diff:
```python
import math

import jax
import jax.numpy as jnp
from jax import lax
from jax.sharding import PartitionSpec as P

two_pi = 2.0 * math.pi


def wave_table(mode_list, first_time, time_count, series_length):
    time_index = first_time + lax.iota(jnp.int32, time_count)
    phases = time_index[:, None] * mode_list[None, :] % series_length
    angles = phases.astype(jnp.float32) * (two_pi / series_length)
    waves = jnp.stack([jnp.cos(angles), -jnp.sin(angles)], axis=2)
    return waves.astype(jnp.bfloat16).reshape(time_count, -1)


def body(series, modes, query_weight, mix_weight, out_weight):
    series_count, shard_rows, model_width = series.shape
    group_width = query_weight.shape[1]
    mode_total = modes.shape[0]
    own_modes, heads_here, head_size, _ = mix_weight.shape
    head_groups = lax.axis_size("head")
    own_series = series_count // head_groups
    series_length = lax.axis_size("tm") * shard_rows
    first_time = lax.axis_index("tm") * shard_rows
    forward_scale = 1.0 / math.sqrt(series_length)
    inverse_scale = 1.0 / math.sqrt(mode_total)
    highest = lax.Precision.HIGHEST
    mine = lax.dynamic_slice_in_dim(series, lax.axis_index("head") * own_series, own_series, 0)
    table = wave_table(modes, first_time, shard_rows, series_length)
    partial = jnp.einsum("tk,btd->kbd", table, mine, preferred_element_type=jnp.float32)
    summed = lax.psum_scatter(partial * forward_scale, "tm", scatter_dimension=0, tiled=True)
    summed = lax.all_gather(summed, "head", axis=1, tiled=True)
    spectrum = jnp.einsum("kbd,df->kbf", summed, query_weight.astype(jnp.float32), precision=highest)
    parts = spectrum.reshape(own_modes, 2, series_count, heads_here, head_size)
    from_real = jnp.einsum("mbhi,mhio->mbho", parts[:, 0], mix_weight, precision=highest)
    from_imag = jnp.einsum("mbhi,mhio->mbho", parts[:, 1], mix_weight, precision=highest)
    mixed_real = from_real[..., :head_size] - from_imag[..., head_size:]
    mixed_imag = from_real[..., head_size:] + from_imag[..., :head_size]
    mixed = jnp.stack([mixed_real, mixed_imag], axis=1).astype(jnp.bfloat16)
    mixed = mixed.reshape(2 * own_modes, series_count, group_width)
    mixed = lax.all_gather(mixed, "head", axis=2, tiled=True)
    projected = jnp.einsum("kbf,fo->kbo", mixed, out_weight, preferred_element_type=jnp.float32)
    projected = (projected * inverse_scale).astype(jnp.bfloat16)
    everything = lax.all_gather(projected, "tm", axis=0, tiled=True)
    output = jnp.einsum("tk,kbo->bto", table, everything, preferred_element_type=jnp.float32)
    return output.astype(jnp.bfloat16)


def solution(mesh):
    in_specs = (
        P(None, "tm", None),
        P(),
        P(None, "head"),
        P("tm", "head", None, None),
        P(None, "head"),
    )
    out_specs = P(None, "tm", "head")
    return jax.shard_map(body, mesh=mesh, in_specs=in_specs, out_specs=out_specs, check_vma=False)
```

time: 307 us -> 476 us (1.55)
  waiting for transfers between devices: 214 us -> 421 us
  matrix products: 38.9 us -> 14.9 us
  local copies, waits for them, and re-layouts: 31 us -> 18.7 us
    reduce_scatter x0 -> x1, waiting for transfers between devices: none -> 360 us  [body(): lax.psum_scatter(partial * forward_scale, 'tm', scatter_dimension=0, tile...]
    psum x1 -> x0, waiting for transfers between devices: 141 us -> none  [body(): lax.psum(jnp.stack([real_part, -imag_part], axis=1) * forward_scale, 'tm')]
    dot_general x7 -> x6, matrix products: 38.9 us -> 14.9 us  [the longest x1 7.48 us: body(): jnp.einsum('tk,kbo->bto', table, everything, preferred_element_type=jnp.f...]
    all_gather x2 -> x1, waiting for transfers between devices: 72.9 us -> 60.4 us  [body(): everything = lax.all_gather(projected, 'tm', axis=0, tiled=True)]
    convert_element_type x1 -> x4, local copies, waits for them, and re-layouts: 21.7 us -> 12.7 us  [the longest x1 12.2 us: body(): return output.astype(jnp.bfloat16)]
  transfers between devices with their start and end apart: 3 -> 2, of which waited for: 3 -> 2; matrix products, arithmetic and copies ran while one was open for 1% -> 0% of each run, Pallas kernels for 0% -> 0%
where the time goes in v1:
time: 476 us; the launch traced here: 475 us
  waiting for transfers between devices  421 us (88%)
  local copies, waits for them, and re-layouts  18.7 us (4%)
  matrix products  14.9 us (3%)
  between operations  13.5 us (3%)
    reduce_scatter x1, waiting for transfers between devices, body(): lax.psum_scatter(partial * forward_scale, 'tm', scatter_dimension=0, tile...  360 us
    all_gather x1, waiting for transfers between devices, body(): everything = lax.all_gather(projected, 'tm', axis=0, tiled=True)  60.4 us
    convert_element_type x1, local copies, waits for them, and re-layouts, body(): return output.astype(jnp.bfloat16)  12.2 us
  transfers between devices with their start and end apart: 2, of which 2 were waited for; matrix products, arithmetic and copies ran while one was open for 0% of the time, Pallas kernels for 0%

profile of v1, /device:TPU:0, one launch (start us, length us, event | category | flops | bytes accessed | tf_op | source)
XLA Modules:
  0.0 475.2 jit_solution(6444277786331292956)
XLA Ops:
  6.5 0.0 copy-start
  6.5 0.0 reduce-scatter.2.cloned.1.call-start
  6.5 3.2 cosine_convert_fusion
  9.7 0.1 pad_maximum_fusion
  9.8 0.5 copy.30
  10.3 0.2 reshape.141
  10.5 5.7 %fusion.2 = f32[256,8,512]{2,0,1:T(8,128)S(1)} fusion(bf16[1024,256,1]{0,1,2:T(8,128)(2,1)S(1)} %reshape.141, bf16[16,1024,512]{2,1,0:T(8,128)(2,1)} %param.5, s32[]{:T(128)S(6)} %select_n.22), kind=kOutput, calls=%fused_computation.3 | convolution fusion | flops 2148532224 | bytes 13107204 | tf_op jit(solution)/shard_map/tk,btd->kbd/dot_general | solution.py:33
  16.3 4.4 copy.31
  20.7 0.0 copy-start.1
  20.7 0.0 copy-start.2
  20.7 0.0 reduce-scatter.2.cloned.1.call-update
  20.7 0.0 all-gather.2.cloned.1.call-start
  20.8 360.5 %reduce-scatter.2.cloned.1.call-done = f32[4,8,512]{2,1,0:T(8,128)} async-done(((f32[256,8,512]{2,1,0:T(8,128)}), f32[4,8,512]{2,1,0:T(8,128)}) %reduce-scatter.2.cloned.1.call-update) | async-done | bytes 65552 | tf_op jit(solution)/shard_map/reduce_scatter | solution.py:34
  381.3 0.9 copy.32
  382.2 1.9 all_gather.9
  384.1 0.0 copy-done.1
  384.1 0.3 fusion.12
  384.3 0.1 reshape.140
  384.5 0.0 copy-done
  384.5 0.3 convolution_bitcast_fusion.1
  384.8 0.3 convolution_bitcast_fusion
  385.1 0.1 fusion.17
  385.3 0.1 convert_element_type.36
  385.4 1.8 all_gather.10
  387.3 0.0 copy-done.2
  387.3 0.8 fusion.6
  388.1 0.0 all-gather.2.cloned.1.call-update
  388.1 0.2 convert_element_type.35
  388.3 60.4 %all-gather.2.cloned.1.call-done = bf16[256,16,256]{2,1,0:T(8,128)(2,1)} async-done(((bf16[4,16,256]{2,1,0:T(8,128)(2,1)}), bf16[256,16,256]{2,1,0:T(8,128)(2,1)}) %all-gather.2.cloned.1.call-update) | async-done | bytes 2097168 | tf_op jit(solution)/shard_map/all_gather | solution.py:47
  448.7 7.5 %convert_bitcast_fusion = bf16[16,1024,256]{1,2,0:T(8,128)(2,1)} fusion(bf16[256,16,256]{2,1,0:T(8,128)(2,1)} %all-gather.2.cloned.1.call-done, bf16[1024,256]{0,1:T(8,128)(2,1)S(1)} %convert_element_type.35), kind=kOutput, calls=%fused_computation | convolution fusion | flops 2151677952 | bytes 11010048 | tf_op jit(solution)/shard_map/tk,kbo->bto/dot_general | solution.py:48
  456.2 12.2 %copy.39 = bf16[16,1024,256]{2,1,0:T(8,128)(2,1)} copy(bf16[16,1024,256]{1,2,0:T(8,128)(2,1)} %convert_bitcast_fusion) | data formatting | bytes 16777216 | tf_op jit(solution)/shard_map/convert_element_type | solution.py:49
  (4 shorter events, 0.1 us)
Async XLA Ops:
  6.5 377.9 %copy-start = (f32[2,4,64,128]{3,2,1,0:T(8,128)S(1)}, f32[2,4,64,128]{3,2,1,0:T(8,128)}, u32[]{:S(2)}) copy-start(f32[2,4,64,128]{3,2,1,0:T(8,128)} %param.8) | copy-start | bytes 786436
  6.5 374.7 %reduce-scatter.2.cloned.1.call-start = ((), (), s32[]{:S(2)}) async-start(), calls=%async_computation.1 | async-start | bytes 4259840 | tf_op jit(solution)/shard_map/reduce_scatter | solution.py:34
  20.7 363.4 %copy-start.1 = (bf16[512,256]{1,0:T(8,128)(2,1)S(1)}, bf16[512,256]{1,0:T(8,128)(2,1)}, u32[]{:S(2)}) copy-start(bf16[512,256]{1,0:T(8,128)(2,1)} %param.7) | copy-start | bytes 786436
  20.7 366.6 %copy-start.2 = (bf16[512,256]{1,0:T(8,128)(2,1)S(1)}, bf16[512,256]{1,0:T(8,128)(2,1)}, u32[]{:S(2)}) copy-start(bf16[512,256]{1,0:T(8,128)(2,1)} %param.9) | copy-start | bytes 786436
  20.7 428.0 %all-gather.2.cloned.1.call-start = ((), (), s32[]{:S(2)}) async-start(), calls=%async_computation.2 | async-start | bytes 2129920 | tf_op jit(solution)/shard_map/all_gather | solution.py:47
Sparse Core Ops, SparseCore 0:
  20.9 360.3 reduce-scatter.1
  388.2 60.4 all-gather.1

commit v2 on v1

v2 whole, which is shorter than its diff:
```python
import functools
import math

import jax
import jax.numpy as jnp
from jax import lax
from jax.experimental import pallas as pl
from jax.experimental.pallas import tpu as pltpu
from jax.sharding import PartitionSpec as P

F32 = jnp.float32
BF16 = jnp.bfloat16
MESH = pl.DeviceIdType.MESH
RING = 4
PARTS = 3
PERIOD = 65536


def iota(shape, dim):
    return lax.broadcasted_iota(jnp.int32, shape, dim)


def one_hot(shape, wanted):
    return (iota(shape, 1) == wanted).astype(F32).astype(BF16)


def dot(a, b):
    return jnp.dot(a, b, preferred_element_type=F32)


def dot_nt(a, b):
    return lax.dot_general(a, b, (((1,), (1,)), ((), ())), preferred_element_type=F32)


def cos_sin(phase):
    phase = phase & (PERIOD - 1)
    quarter = (phase + PERIOD // 8) >> 14
    r = (phase - (quarter << 14)).astype(F32) * (2.0 * math.pi / PERIOD)
    q = r * r
    s = r * (1.0 + q * (-1 / 6 + q * (1 / 120 + q * (-1 / 5040 + q * (1 / 362880)))))
    c = 1.0 + q * (-0.5 + q * (1 / 24 + q * (-1 / 720 + q * (1 / 40320))))
    odd = (quarter & 1) == 1
    cos_value = jnp.where(odd, s, c)
    sin_value = jnp.where(odd, c, s)
    cos_value = jnp.where(((quarter + 1) & 2) != 0, -cos_value, cos_value)
    sin_value = jnp.where((quarter & 2) != 0, -sin_value, sin_value)
    return cos_value, sin_value


def stride_of(axis):
    return 16 - 12 * axis + 9 * ((axis * (axis - 1)) // 2)


def split(x):
    high = x.astype(BF16)
    low = (x - high.astype(F32)).astype(BF16)
    return high, low


def order_row(k, part):
    first, second, third, r = k // 64, (k // 16) % 4, (k // 4) % 4, k % 4
    if part == 0:
        return k
    if part == 1:
        return third * 64 + first * 16 + second * 4 + r
    return second * 64 + third * 16 + first * 4 + r


def exchange_kernel(
    scale, series, modes, wq_in, mix_in, wo_in, tab_out, gat_out,
    x, table, wide, sent, ra, rb, acc, s2, r2, v3, s3, r3, xs, wq, mix, wo, mw, mx, a1, gb,
    x_sem, w_sem, o_sem, p_send, p_recv, send1, recv1, send2, recv2, send3, recv3,
    g1_send, g1_recv, g2_send, g2_recv, g3_send, g3_recv,
):
    tm = lax.axis_index("tm")
    h = lax.axis_index("head")
    count = x.shape[0]

    def coord(axis):
        return lax.rem(lax.div(tm, stride_of(axis)), RING)

    def along(axis, distance):
        c = coord(axis)
        return tm + (lax.rem(c + distance, RING) - c) * stride_of(axis)

    def remote(src, dst, ssem, rsem, target):
        return pltpu.make_async_remote_copy(
            src_ref=src, dst_ref=dst, send_sem=ssem, recv_sem=rsem,
            device_id=(target, h), device_id_type=MESH,
        )

    def to_partner(src, dst, k):
        return pltpu.make_async_remote_copy(
            src_ref=src, dst_ref=dst, send_sem=p_send.at[k], recv_sem=p_recv.at[k],
            device_id=(tm, 1 - h), device_id_type=MESH,
        )

    def load_x(s):
        return pltpu.make_async_copy(series.at[h * count + s], x.at[s], x_sem.at[s])

    loads = [
        pltpu.make_async_copy(wq_in, wq.at[0], w_sem.at[0]),
        pltpu.make_async_copy(mix_in, mix.at[0], w_sem.at[1]),
        pltpu.make_async_copy(wo_in, wo, w_sem.at[2]),
    ]

    barrier = pltpu.get_barrier_semaphore()
    for axis in range(3):
        for d in range(1, RING):
            pl.semaphore_signal(barrier, inc=1, device_id=(along(axis, d), h), device_id_type=MESH)
    pl.semaphore_signal(barrier, inc=1, device_id=(tm, 1 - h), device_id_type=MESH)

    for s in range(count):
        load_x(s).start()
    for load in loads:
        load.start()

    rows = 256
    steps = x.shape[1]
    blocks = steps // 128
    first = tm * steps
    mode_high = jnp.broadcast_to((modes[...] >> 7).astype(F32), (128, 128)).astype(BF16)
    mode_low = jnp.broadcast_to((modes[...] & 127).astype(F32), (128, 128)).astype(BF16)
    pick = one_hot((rows, 128), iota((rows, 128), 0) // 2)
    by_row = (dot_nt(pick, mode_high) * 128.0 + dot_nt(pick, mode_low)).astype(jnp.int32)
    quarter_turn = (iota((rows, 128), 0) & 1) * (PERIOD // 4)
    cos_low, sin_low = cos_sin(by_row * iota((rows, 128), 1))
    cos_high, sin_high = cos_sin(
        by_row * (first + 128 * (iota((rows, 128), 1) & (blocks - 1))) + quarter_turn
    )
    for i in range(blocks):
        value = cos_high[:, i : i + 1] * cos_low - sin_high[:, i : i + 1] * sin_low
        table[0, :, pl.ds(128 * i, 128)] = value.astype(BF16)
    for part in range(1, PARTS):
        perm = one_hot((rows, rows), order_row(iota((rows, rows), 0), part))
        table[part] = dot(perm, table[0]).astype(BF16)

    pl.semaphore_wait(barrier, 10)
    to_partner(wq_in, wq.at[1], 0).start()
    to_partner(mix_in, mix.at[1], 1).start()

    def band(axis, d):
        c = lax.rem(coord(axis) + d, RING)
        return pl.ds(pl.multiple_of(c * 64, 64), 64)

    def stage1(s, way, kind):
        axis = lax.rem(s, PARTS)
        near = 1 if way == 0 else 3
        mine = pl.ds(256 * way, 256)
        other = pl.ds(256 * (1 - way), 256)
        slot = 2 * kind + way
        if kind == 0:
            src, dst = sent.at[s, band(axis, 2), mine], ra.at[s, way]
        elif kind == 1:
            src, dst = sent.at[s, band(axis, near), other], rb.at[s, way, :, other]
        else:
            src, dst = acc.at[s, way], rb.at[s, way, :, mine]
        return remote(src, dst, send1.at[s, slot], recv1.at[s, slot], along(axis, near))

    def forward(s, carry):
        load_x(s).wait()
        sent[s] = dot(table[lax.rem(s, PARTS)], x[s]).astype(BF16)
        for kind in range(2):
            for way in range(2):
                stage1(s, way, kind).start()
        return carry

    lax.fori_loop(0, count, forward, 0)

    def relay(s, carry):
        axis = lax.rem(s, PARTS)
        for way in range(2):
            stage1(s, way, 0).wait_recv()
            own = sent[s, band(axis, 1 if way == 0 else 3), pl.ds(256 * way, 256)]
            acc[s, way] = (own.astype(F32) + ra[s, way].astype(F32)).astype(BF16)
            stage1(s, way, 2).start()
        return carry

    lax.fori_loop(0, count, relay, 0)

    by_lane = (
        dot_nt(mode_high[0:8], pick) * 128.0 + dot_nt(mode_low[0:8], pick)
    ).astype(jnp.int32)
    turn_lane = (iota((8, rows), 1) & 1) * (PERIOD // 4)
    wide_cos, wide_sin = cos_sin(jnp.broadcast_to(by_lane[0:1], (128, rows)) * iota((128, rows), 0))
    top_cos, top_sin = cos_sin(by_lane * (first + 128 * (iota((8, rows), 0) & (blocks - 1))) + turn_lane)
    for i in range(blocks):
        value = top_cos[i : i + 1] * wide_cos - top_sin[i : i + 1] * wide_sin
        wide[0, pl.ds(128 * i, 128), :] = value.astype(BF16)
    for part in range(1, PARTS):
        perm = one_hot((rows, rows), order_row(iota((rows, rows), 0), part))
        wide[part] = dot_nt(wide[0], perm).astype(BF16)
    table_copy = pltpu.make_async_copy(wide, tab_out, o_sem.at[0])
    table_copy.start()

    for load in loads:
        load.wait()
    to_partner(wq_in, wq.at[1], 0).wait_recv()
    to_partner(mix_in, mix.at[1], 1).wait_recv()
    mw[...] = jnp.zeros_like(mw)
    left = iota((64, 128), 1) < 64
    for half in range(2):
        for m in range(2):
            for head in range(4):
                both = mix[half, m, head]
                turned = pltpu.roll(both, 64, 1)
                for kind in range(2):
                    value = both if kind == head % 2 else turned
                    keep = left if head % 2 == 0 else jnp.logical_not(left)
                    value = jnp.where(keep, value, 0.0).astype(BF16)
                    mw[half, pl.ds((2 * m + kind) * 256 + 64 * head, 64), pl.ds(128 * (head // 2), 128)] = value
    v3[...] = jnp.zeros_like(v3)

    def stage2(s, d):
        axis = lax.rem(s + 1, PARTS)
        c = lax.rem(coord(axis) + d, RING)
        return remote(
            s2.at[s, pl.ds(pl.multiple_of(c * 16, 16), 16), :], r2.at[s, d - 1],
            send2.at[s, d - 1], recv2.at[s, d - 1], along(axis, d),
        )

    def reduce1(s, carry):
        axis = lax.rem(s, PARTS)
        for kind in range(1, 3):
            for way in range(2):
                stage1(s, way, kind).wait_recv()
        total = sent[s, band(axis, 0), :].astype(F32) + rb[s, 0].astype(F32) + rb[s, 1].astype(F32)
        s2[s] = total.astype(BF16)
        for d in range(1, RING):
            stage2(s, d).start()
        return carry

    lax.fori_loop(0, count, reduce1, 0)

    def reduce2(s, carry):
        axis = lax.rem(s + 1, PARTS)
        for d in range(1, RING):
            stage2(s, d).wait_recv()
        own = s2[s, pl.ds(pl.multiple_of(coord(axis) * 16, 16), 16), :].astype(F32)
        total = own + r2[s, 0].astype(F32) + r2[s, 1].astype(F32) + r2[s, 2].astype(F32)
        row = pl.multiple_of(lax.div(s, PARTS) * 16, 16)
        v3[lax.rem(s, PARTS), pl.ds(row, 16), :] = total.astype(BF16)
        return carry

    lax.fori_loop(0, count, reduce2, 0)

    def stage3(part, d):
        axis = (part + 2) % PARTS
        c = lax.rem(coord(axis) + d, RING)
        return remote(
            s3.at[part, c], r3.at[part, d - 1],
            send3.at[part, d - 1], recv3.at[part, d - 1], along(axis, d),
        )

    k = iota((64, 64), 0)
    swap = one_hot((64, 64), ((k // 4) % 4) * 16 + (k // 16) * 4 + k % 4)
    for part in range(PARTS):
        turned = dot(swap, v3[part]).astype(BF16)
        for c in range(RING):
            s3[part, c] = turned[16 * c : 16 * c + 16]
        for d in range(1, RING):
            stage3(part, d).start()
    for part in range(PARTS):
        for d in range(1, RING):
            stage3(part, d).wait_recv()
        own = s3[part, coord((part + 2) % PARTS)].astype(F32)
        xs[pl.ds(16 * part, 16), :] = (
            own + r3[part, 0].astype(F32) + r3[part, 1].astype(F32) + r3[part, 2].astype(F32)
        )

    lhs = jnp.concatenate(split(xs[...]), axis=0)
    held = 16 * PARTS
    odd = (iota((held, 256), 0) & 1) == 1
    second = (iota((held, 256), 0) & 2) == 2
    for half in range(2):
        q = dot(lhs, wq[half])
        q = q[:held] + q[held:]
        crossed = jnp.where(odd, pltpu.roll(q, 1, 0), -pltpu.roll(q, held - 1, 0))
        pieces = [
            jnp.where(second, 0.0, q), jnp.where(second, 0.0, crossed),
            jnp.where(second, q, 0.0), jnp.where(second, crossed, 0.0),
        ]
        mixed = jnp.zeros((2 * held, 256), F32)
        for i in range(4):
            mixed = mixed + dot(jnp.concatenate(split(pieces[i]), axis=0), mw[half, pl.ds(256 * i, 256), :])
        mixed = (mixed[:held] + mixed[held:]).astype(BF16)
        mx[h, h if half == 0 else 1 - h] = mixed
    to_partner(mx.at[h], mx.at[h], 2).start()
    to_partner(mx.at[h], mx.at[h], 2).wait_recv()

    def gather1(part, d):
        axis = (part + 2) % PARTS
        c = coord(axis)
        return remote(
            a1.at[part, c], a1.at[part, c],
            g1_send.at[part, d - 1], g1_recv.at[part, d - 1], along(axis, d),
        )

    for group in range(2):
        g = dot(mx[group, 0], wo[pl.ds(0, 256), :]) + dot(mx[group, 1], wo[pl.ds(256, 256), :])
        g = (g * scale).astype(BF16)
        for part in range(PARTS):
            a1[part, coord((part + 2) % PARTS), pl.ds(16 * group, 16), :] = g[16 * part : 16 * part + 16]
    for part in range(PARTS):
        for d in range(1, RING):
            gather1(part, d).start()

    def spot(part, second_shift, first_shift=0):
        c1 = lax.rem(coord(part) + first_shift, RING)
        c2 = lax.rem(coord((part + 1) % PARTS) + second_shift, RING)
        return pl.ds(pl.multiple_of(c1 * 64 + c2 * 16, 16), 16)

    def gather2(part, d):
        return remote(
            gb.at[part, :, :, spot(part, 0), :], gb.at[part, :, :, spot(part, 0), :],
            g2_send.at[part, d - 1], g2_recv.at[part, d - 1], along((part + 1) % PARTS, d),
        )

    k = iota((96, 128), 0)
    unswap = one_hot((96, 128), ((k // 4) % 4) * 32 + (k // 48) * 16 + ((k // 16) % 3) * 4 + k % 4)
    for part in range(PARTS):
        for d in range(1, RING):
            gather1(part, d).wait_recv()
        flat = jnp.concatenate([a1[part, c] for c in range(RING)], axis=0)
        turned = dot(unswap, flat).astype(BF16)
        for group in range(2):
            for j in range(PARTS):
                at = 48 * group + 16 * j
                gb[part, group, j, spot(part, 0), :] = turned[at : at + 16]
        for d in range(1, RING):
            gather2(part, d).start()

    def gather3(part, way, group, relayed):
        near = 1 if way == 0 else 3
        c = lax.rem(coord(part) + (RING - near if relayed else 0), RING)
        at = gb.at[part, group, :, pl.ds(pl.multiple_of(c * 64, 64), 64), :]
        slot = 2 if relayed else group
        return remote(at, at, g3_send.at[part, way, slot], g3_recv.at[part, way, slot], along(part, near))

    for part in range(PARTS):
        for d in range(1, RING):
            gather2(part, d).wait_recv()
        for turn in range(2):
            for way in range(2):
                gather3(part, way, turn if way == 0 else 1 - turn, False).start()
    for part in range(PARTS):
        for way in range(2):
            gather3(part, way, way, False).wait_recv()
            gather3(part, way, way, True).start()
    gathered = []
    for part in range(PARTS):
        for way in range(2):
            gather3(part, way, 1 - way, False).wait_recv()
        for way in range(2):
            gather3(part, way, way, True).wait_recv()
        copy = pltpu.make_async_copy(gb.at[part], gat_out.at[part], o_sem.at[1 + part])
        copy.start()
        gathered.append(copy)

    def drain(s, carry):
        for kind in range(3):
            for way in range(2):
                stage1(s, way, kind).wait_send()
        for d in range(1, RING):
            stage2(s, d).wait_send()
        return carry

    lax.fori_loop(0, count, drain, 0)
    to_partner(wq_in, wq.at[1], 0).wait_send()
    to_partner(mix_in, mix.at[1], 1).wait_send()
    to_partner(mx.at[h], mx.at[h], 2).wait_send()
    for part in range(PARTS):
        for d in range(1, RING):
            stage3(part, d).wait_send()
            gather1(part, d).wait_send()
            gather2(part, d).wait_send()
        for way in range(2):
            gather3(part, way, 0, False).wait_send()
            gather3(part, way, 1, False).wait_send()
            gather3(part, way, way, True).wait_send()
    table_copy.wait()
    for copy in gathered:
        copy.wait()


def inverse_kernel(table, gathered, out):
    out[...] = dot(table[...], gathered[...]).astype(BF16)


def place(step):
    part = step // 6
    depth = 3 - part // 2
    left = step % 6
    return part, left // depth, left % depth


def body(series, modes, query_weight, mix_weight, out_weight):
    series_count, steps, width = series.shape
    group = query_weight.shape[1]
    count = series_count // 2
    scale = 1.0 / math.sqrt(PERIOD) / math.sqrt(modes.shape[0])
    any_space = pl.BlockSpec(memory_space=pl.ANY)
    dma = pltpu.SemaphoreType.DMA
    vm = pltpu.VMEM
    tables, gathered = pl.pallas_call(
        functools.partial(exchange_kernel, scale),
        out_shape=(
            jax.ShapeDtypeStruct((PARTS, steps, 256), BF16),
            jax.ShapeDtypeStruct((PARTS, 2, 3, 256, group), BF16),
        ),
        in_specs=[any_space, pl.BlockSpec(memory_space=pltpu.VMEM), any_space, any_space, any_space],
        out_specs=(any_space, any_space),
        scratch_shapes=[
            vm((count, steps, width), BF16),
            vm((PARTS, 256, steps), BF16),
            vm((PARTS, steps, 256), BF16),
            vm((count, 256, width), BF16),
            vm((count, 2, 64, 256), BF16),
            vm((count, 2, 64, width), BF16),
            vm((count, 2, 64, 256), BF16),
            vm((count, 64, width), BF16),
            vm((count, 3, 16, width), BF16),
            vm((PARTS, 64, width), BF16),
            vm((PARTS, RING, 16, width), BF16),
            vm((PARTS, 3, 16, width), BF16),
            vm((48, width), F32),
            vm((2, width, group), BF16),
            vm((2,) + mix_weight.shape, F32),
            vm((width, group), BF16),
            vm((2, 1024, 256), BF16),
            vm((2, 2, 48, 256), BF16),
            vm((PARTS, RING, 32, group), BF16),
            vm((PARTS, 2, 3, 256, group), BF16),
            dma((count,)), dma((3,)), dma((4,)), dma((3,)), dma((3,)),
            dma((count, 6)), dma((count, 6)), dma((count, 3)), dma((count, 3)),
            dma((PARTS, 3)), dma((PARTS, 3)),
            dma((PARTS, 3)), dma((PARTS, 3)), dma((PARTS, 3)), dma((PARTS, 3)),
            dma((PARTS, 2, 3)), dma((PARTS, 2, 3)),
        ],
        compiler_params=pltpu.CompilerParams(
            collective_id=0, has_side_effects=True, vmem_limit_bytes=60 * 1024 * 1024
        ),
        name="exchange",
    )(series, modes.reshape(1, -1), query_weight, mix_weight, out_weight)

    return pl.pallas_call(
        inverse_kernel,
        grid=(series_count,),
        out_shape=jax.ShapeDtypeStruct((series_count, steps, group), BF16),
        in_specs=[
            pl.BlockSpec((None, steps, 256), lambda i: (place(i)[0], 0, 0)),
            pl.BlockSpec((None, None, None, 256, group), lambda i: place(i) + (0, 0)),
        ],
        out_specs=pl.BlockSpec(
            (None, steps, group), lambda i: (place(i)[1] * 8 + 3 * place(i)[2] + place(i)[0], 0, 0)
        ),
        name="inverse",
    )(tables, gathered)


def solution(mesh):
    in_specs = (
        P(None, "tm", None),
        P(),
        P(None, "head"),
        P("tm", "head", None, None),
        P(None, "head"),
    )
    out_specs = P(None, "tm", "head")
    return jax.shard_map(body, mesh=mesh, in_specs=in_specs, out_specs=out_specs, check_vma=False)
```

time: 476 us -> 62.4 us (0.13)
  waiting for transfers between devices: 421 us -> 0 us
  Pallas kernels: 0 us -> 62 us
  local copies, waits for them, and re-layouts: 18.7 us -> 0 us
  matrix products: 14.9 us -> 0 us
  between operations: 13.5 us -> 0.01 us
    reduce_scatter x1 -> x0, waiting for transfers between devices: 360 us -> none  [body(): lax.psum_scatter(partial * forward_scale, 'tm', scatter_dimension=0, tile...]
    pallas_call x0 -> x2, Pallas kernels: none -> 62 us  [the longest x1 48.9 us: body(): pl.pallas_call(functools.partial(exchange_kernel, scale), out_shape=(jax....]
    all_gather x1 -> x0, waiting for transfers between devices: 60.4 us -> none  [body(): everything = lax.all_gather(projected, 'tm', axis=0, tiled=True)]
    dot_general x6 -> x0, matrix products: 14.9 us -> none  [the longest x1 7.48 us: body(): jnp.einsum('tk,kbo->bto', table, everything, preferred_element_type=jnp.f...]
    convert_element_type x4 -> x0, local copies, waits for them, and re-layouts: 12.7 us -> none  [the longest x1 12.2 us: body(): return output.astype(jnp.bfloat16)]
  transfers between devices with their start and end apart: 2 -> 0, of which waited for: 2 -> 0; matrix products, arithmetic and copies ran while one was open for 0% -> 0% of each run, Pallas kernels for 0% -> 0%
where the time goes in v2:
time: 62.4 us; the launch traced here: 62 us
  Pallas kernels  62 us (99%)
    pallas_call x1, Pallas kernels, body(): pl.pallas_call(functools.partial(exchange_kernel, scale), out_shape=(jax....  48.9 us
    pallas_call x1, Pallas kernels, body(): pl.pallas_call(inverse_kernel, grid=(series_count,), out_shape=jax.ShapeD...  13 us

profile of v2, /device:TPU:0, one launch (start us, length us, event | category | flops | bytes accessed | tf_op | source)
XLA Modules:
  0.0 62.0 jit_solution(14831334758205628782)
XLA Ops:
  0.0 48.9 %exchange.1 = (bf16[3,1024,256]{2,1,0:T(8,128)(2,1)}, bf16[3,2,3,256,256]{4,3,2,1,0:T(8,128)(2,1)}) custom-call(bf16[16,1024,512]{2,1,0:T(8,128)(2,1)} %series.1, s32[1,128]{1,0:T(1,128)} %bitcast.1, bf16[512,256]{1,0:T(8,128)(2,1)} %wq_in.1, f32[2,4,64,128]{3,2,1,0:T(8,128)} %mix_in.1, bf16[512,256]{1,0:T(8,128)(2,1)} %wo_in.1), custom_call_target="tpu_custom_call" | custom-call | tf_op jit(solution)/shard_map/exchange/pallas_call | solution.py:405
  48.9 13.0 %inverse.1 = bf16[16,1024,256]{2,1,0:T(8,128)(2,1)} custom-call(bf16[3,1024,256]{2,1,0:T(8,128)(2,1)} %get-tuple-element.7.table, bf16[3,2,3,256,256]{4,3,2,1,0:T(8,128)(2,1)} %get-tuple-element.8.gathered), custom_call_target="tpu_custom_call" | custom-call | tf_op jit(solution)/shard_map/inverse/pallas_call | solution.py:446

commit v3 on v2

--- a/solution.py
+++ b/solution.py
@@ -383,15 +383,37 @@
         copy.wait()
 
 
-def inverse_kernel(table, gathered, out):
-    out[...] = dot(table[...], gathered[...]).astype(BF16)
-
-
-def place(step):
-    part = step // 6
-    depth = 3 - part // 2
-    left = step % 6
-    return part, left // depth, left % depth
+def inverse_kernel(tab_in, gat_in, out, tab, gat, res, t_sem, g_sem, o_sem):
+    def load_tab(part):
+        return pltpu.make_async_copy(tab_in.at[part], tab.at[part], t_sem.at[part])
+
+    def load_gat(part):
+        return pltpu.make_async_copy(gat_in.at[part], gat.at[part], g_sem.at[part])
+
+    def store(s):
+        return pltpu.make_async_copy(res.at[s], out.at[s], o_sem.at[s])
+
+    for part in range(PARTS):
+        load_tab(part).start()
+        load_gat(part).start()
+    for part in range(PARTS):
+        load_tab(part).wait()
+        load_gat(part).wait()
+
+        def step(j, carry):
+            for group in range(2):
+                s = 8 * group + 3 * j + part
+                res[s] = dot(tab[part], gat[part, group, j]).astype(BF16)
+                store(s).start()
+            return carry
+
+        lax.fori_loop(0, 3 - part // 2, step, 0)
+
+    def drain(s, carry):
+        store(s).wait()
+        return carry
+
+    lax.fori_loop(0, out.shape[0], drain, 0)
 
 
 def body(series, modes, query_weight, mix_weight, out_weight):
@@ -445,15 +467,16 @@
 
     return pl.pallas_call(
         inverse_kernel,
-        grid=(series_count,),
         out_shape=jax.ShapeDtypeStruct((series_count, steps, group), BF16),
-        in_specs=[
-            pl.BlockSpec((None, steps, 256), lambda i: (place(i)[0], 0, 0)),
-            pl.BlockSpec((None, None, None, 256, group), lambda i: place(i) + (0, 0)),
+        in_specs=[any_space, any_space],
+        out_specs=any_space,
+        scratch_shapes=[
+            vm((PARTS, steps, 256), BF16),
+            vm((PARTS, 2, 3, 256, group), BF16),
+            vm((series_count, steps, group), BF16),
+            dma((PARTS,)), dma((PARTS,)), dma((series_count,)),
         ],
-        out_specs=pl.BlockSpec(
-            (None, steps, group), lambda i: (place(i)[1] * 8 + 3 * place(i)[2] + place(i)[0], 0, 0)
-        ),
+        compiler_params=pltpu.CompilerParams(vmem_limit_bytes=60 * 1024 * 1024),
         name="inverse",
     )(tables, gathered)
 

time: 62.4 us -> 55.3 us (0.89)
  Pallas kernels: 62 us -> 55.2 us
    pallas_call x1, Pallas kernels: 13 us -> 6.24 us  [body(): pl.pallas_call(inverse_kernel, out_shape=jax.ShapeDtypeStruct((series_cou...]
where the time goes in v3:
time: 55.3 us; the launch traced here: 55.2 us
  Pallas kernels  55.2 us (100%)
    pallas_call x1, Pallas kernels, body(): pl.pallas_call(functools.partial(exchange_kernel, scale), out_shape=(jax....  48.9 us
    pallas_call x1, Pallas kernels, body(): pl.pallas_call(inverse_kernel, out_shape=jax.ShapeDtypeStruct((series_cou...  6.24 us

profile of v3, /device:TPU:0, one launch (start us, length us, event | category | flops | bytes accessed | tf_op | source)
XLA Modules:
  0.0 55.2 jit_solution(14128556333098530548)
XLA Ops:
  0.0 48.9 %exchange.1 = (bf16[3,1024,256]{2,1,0:T(8,128)(2,1)}, bf16[3,2,3,256,256]{4,3,2,1,0:T(8,128)(2,1)}) custom-call(bf16[16,1024,512]{2,1,0:T(8,128)(2,1)} %series.1, s32[1,128]{1,0:T(1,128)} %bitcast.1, bf16[512,256]{1,0:T(8,128)(2,1)} %wq_in.1, f32[2,4,64,128]{3,2,1,0:T(8,128)} %mix_in.1, bf16[512,256]{1,0:T(8,128)(2,1)} %wo_in.1), custom_call_target="tpu_custom_call" | custom-call | tf_op jit(solution)/shard_map/exchange/pallas_call | solution.py:427
  48.9 6.2 %inverse.1 = bf16[16,1024,256]{2,1,0:T(8,128)(2,1)} custom-call(bf16[3,1024,256]{2,1,0:T(8,128)(2,1)} %get-tuple-element.7.tab_in, bf16[3,2,3,256,256]{4,3,2,1,0:T(8,128)(2,1)} %get-tuple-element.8.gat_in), custom_call_target="tpu_custom_call" | custom-call | tf_op jit(solution)/shard_map/inverse/pallas_call | solution.py:468

commit v4 on v3

--- a/solution.py
+++ b/solution.py
@@ -316,6 +316,15 @@
             g2_send.at[part, d - 1], g2_recv.at[part, d - 1], along((part + 1) % PARTS, d),
         )
 
+    def gather3(part, way, piece, relayed):
+        near = 1 if way == 0 else 3
+        if relayed:
+            at = gb.at[part, way, :, spot(part, piece, RING - near), :]
+        else:
+            at = gb.at[part, :, :, spot(part, piece), :]
+        slot = piece + (RING if relayed else 0)
+        return remote(at, at, g3_send.at[part, way, slot], g3_recv.at[part, way, slot], along(part, near))
+
     k = iota((96, 128), 0)
     unswap = one_hot((96, 128), ((k // 4) % 4) * 32 + (k // 48) * 16 + ((k // 16) % 3) * 4 + k % 4)
     for part in range(PARTS):
@@ -329,30 +338,29 @@
                 gb[part, group, j, spot(part, 0), :] = turned[at : at + 16]
         for d in range(1, RING):
             gather2(part, d).start()
-
-    def gather3(part, way, group, relayed):
-        near = 1 if way == 0 else 3
-        c = lax.rem(coord(part) + (RING - near if relayed else 0), RING)
-        at = gb.at[part, group, :, pl.ds(pl.multiple_of(c * 64, 64), 64), :]
-        slot = 2 if relayed else group
-        return remote(at, at, g3_send.at[part, way, slot], g3_recv.at[part, way, slot], along(part, near))
-
-    for part in range(PARTS):
-        for d in range(1, RING):
+        for way in range(2):
+            gather3(part, way, 0, False).start()
+
+    def relay3(piece):
+        for part in range(PARTS):
+            for way in range(2):
+                gather3(part, way, piece, False).wait_recv()
+                gather3(part, way, piece, True).start()
+
+    relayed = 0
+    for d in (1, 3, 2):
+        for part in range(PARTS):
             gather2(part, d).wait_recv()
-        for turn in range(2):
             for way in range(2):
-                gather3(part, way, turn if way == 0 else 1 - turn, False).start()
+                gather3(part, way, RING - d, False).start()
+        relay3(relayed)
+        relayed = RING - d
+    relay3(relayed)
+    gathered = []
     for part in range(PARTS):
         for way in range(2):
-            gather3(part, way, way, False).wait_recv()
-            gather3(part, way, way, True).start()
-    gathered = []
-    for part in range(PARTS):
-        for way in range(2):
-            gather3(part, way, 1 - way, False).wait_recv()
-        for way in range(2):
-            gather3(part, way, way, True).wait_recv()
+            for piece in range(RING):
+                gather3(part, way, piece, True).wait_recv()
         copy = pltpu.make_async_copy(gb.at[part], gat_out.at[part], o_sem.at[1 + part])
         copy.start()
         gathered.append(copy)
@@ -375,9 +383,9 @@
             gather1(part, d).wait_send()
             gather2(part, d).wait_send()
         for way in range(2):
-            gather3(part, way, 0, False).wait_send()
-            gather3(part, way, 1, False).wait_send()
-            gather3(part, way, way, True).wait_send()
+            for piece in range(RING):
+                gather3(part, way, piece, False).wait_send()
+                gather3(part, way, piece, True).wait_send()
     table_copy.wait()
     for copy in gathered:
         copy.wait()
@@ -457,7 +465,7 @@
             dma((count, 6)), dma((count, 6)), dma((count, 3)), dma((count, 3)),
             dma((PARTS, 3)), dma((PARTS, 3)),
             dma((PARTS, 3)), dma((PARTS, 3)), dma((PARTS, 3)), dma((PARTS, 3)),
-            dma((PARTS, 2, 3)), dma((PARTS, 2, 3)),
+            dma((PARTS, 2, 2 * RING)), dma((PARTS, 2, 2 * RING)),
         ],
         compiler_params=pltpu.CompilerParams(
             collective_id=0, has_side_effects=True, vmem_limit_bytes=60 * 1024 * 1024

time: 55.3 us -> 57.5 us (1.040)
  Pallas kernels: 55.2 us -> 57.4 us
    pallas_call x1, Pallas kernels: 48.9 us -> 51.1 us  [body(): pl.pallas_call(functools.partial(exchange_kernel, scale), out_shape=(jax....]
where the time goes in v4:
time: 57.5 us; the launch traced here: 57.4 us
  Pallas kernels  57.4 us (100%)
    pallas_call x1, Pallas kernels, body(): pl.pallas_call(functools.partial(exchange_kernel, scale), out_shape=(jax....  51.1 us
    pallas_call x1, Pallas kernels, body(): pl.pallas_call(inverse_kernel, out_shape=jax.ShapeDtypeStruct((series_cou...  6.24 us

profile of v4, /device:TPU:0, one launch (start us, length us, event | category | flops | bytes accessed | tf_op | source)
XLA Modules:
  0.0 57.4 jit_solution(867722257547016979)
XLA Ops:
  0.0 51.1 %exchange.1 = (bf16[3,1024,256]{2,1,0:T(8,128)(2,1)}, bf16[3,2,3,256,256]{4,3,2,1,0:T(8,128)(2,1)}) custom-call(bf16[16,1024,512]{2,1,0:T(8,128)(2,1)} %series.1, s32[1,128]{1,0:T(1,128)} %bitcast.1, bf16[512,256]{1,0:T(8,128)(2,1)} %wq_in.1, f32[2,4,64,128]{3,2,1,0:T(8,128)} %mix_in.1, bf16[512,256]{1,0:T(8,128)(2,1)} %wo_in.1), custom_call_target="tpu_custom_call" | custom-call | tf_op jit(solution)/shard_map/exchange/pallas_call | solution.py:435
  51.2 6.2 %inverse.1 = bf16[16,1024,256]{2,1,0:T(8,128)(2,1)} custom-call(bf16[3,1024,256]{2,1,0:T(8,128)(2,1)} %get-tuple-element.7.tab_in, bf16[3,2,3,256,256]{4,3,2,1,0:T(8,128)(2,1)} %get-tuple-element.8.gat_in), custom_call_target="tpu_custom_call" | custom-call | tf_op jit(solution)/shard_map/inverse/pallas_call | solution.py:476

commit v5 on v3

--- a/solution.py
+++ b/solution.py
@@ -305,14 +305,10 @@
         for d in range(1, RING):
             gather1(part, d).start()
 
-    def spot(part, second_shift, first_shift=0):
-        c1 = lax.rem(coord(part) + first_shift, RING)
-        c2 = lax.rem(coord((part + 1) % PARTS) + second_shift, RING)
-        return pl.ds(pl.multiple_of(c1 * 64 + c2 * 16, 16), 16)
-
     def gather2(part, d):
+        at = gb.at[part, coord(part), :, coord((part + 1) % PARTS)]
         return remote(
-            gb.at[part, :, :, spot(part, 0), :], gb.at[part, :, :, spot(part, 0), :],
+            at, at,
             g2_send.at[part, d - 1], g2_recv.at[part, d - 1], along((part + 1) % PARTS, d),
         )
 
@@ -326,14 +322,14 @@
         for group in range(2):
             for j in range(PARTS):
                 at = 48 * group + 16 * j
-                gb[part, group, j, spot(part, 0), :] = turned[at : at + 16]
+                gb[part, coord(part), group, coord((part + 1) % PARTS), j] = turned[at : at + 16]
         for d in range(1, RING):
             gather2(part, d).start()
 
     def gather3(part, way, group, relayed):
         near = 1 if way == 0 else 3
         c = lax.rem(coord(part) + (RING - near if relayed else 0), RING)
-        at = gb.at[part, group, :, pl.ds(pl.multiple_of(c * 64, 64), 64), :]
+        at = gb.at[part, c, group]
         slot = 2 if relayed else group
         return remote(at, at, g3_send.at[part, way, slot], g3_recv.at[part, way, slot], along(part, near))
 
@@ -403,7 +399,8 @@
         def step(j, carry):
             for group in range(2):
                 s = 8 * group + 3 * j + part
-                res[s] = dot(tab[part], gat[part, group, j]).astype(BF16)
+                waves = gat[part, :, group, :, j].reshape(256, gat.shape[-1])
+                res[s] = dot(tab[part], waves).astype(BF16)
                 store(s).start()
             return carry
 
@@ -421,6 +418,7 @@
     group = query_weight.shape[1]
     count = series_count // 2
     scale = 1.0 / math.sqrt(PERIOD) / math.sqrt(modes.shape[0])
+    hbm = pl.BlockSpec(memory_space=pltpu.HBM)
     any_space = pl.BlockSpec(memory_space=pl.ANY)
     dma = pltpu.SemaphoreType.DMA
     vm = pltpu.VMEM
@@ -428,9 +426,9 @@
         functools.partial(exchange_kernel, scale),
         out_shape=(
             jax.ShapeDtypeStruct((PARTS, steps, 256), BF16),
-            jax.ShapeDtypeStruct((PARTS, 2, 3, 256, group), BF16),
+            jax.ShapeDtypeStruct((PARTS, RING, 2, RING, 3, 16, group), BF16),
         ),
-        in_specs=[any_space, pl.BlockSpec(memory_space=pltpu.VMEM), any_space, any_space, any_space],
+        in_specs=[hbm, pl.BlockSpec(memory_space=pltpu.VMEM), hbm, hbm, hbm],
         out_specs=(any_space, any_space),
         scratch_shapes=[
             vm((count, steps, width), BF16),
@@ -452,7 +450,7 @@
             vm((2, 1024, 256), BF16),
             vm((2, 2, 48, 256), BF16),
             vm((PARTS, RING, 32, group), BF16),
-            vm((PARTS, 2, 3, 256, group), BF16),
+            vm((PARTS, RING, 2, RING, 3, 16, group), BF16),
             dma((count,)), dma((3,)), dma((4,)), dma((3,)), dma((3,)),
             dma((count, 6)), dma((count, 6)), dma((count, 3)), dma((count, 3)),
             dma((PARTS, 3)), dma((PARTS, 3)),
@@ -460,7 +458,7 @@
             dma((PARTS, 2, 3)), dma((PARTS, 2, 3)),
         ],
         compiler_params=pltpu.CompilerParams(
-            collective_id=0, has_side_effects=True, vmem_limit_bytes=60 * 1024 * 1024
+            collective_id=0, has_side_effects=True, vmem_limit_bytes=50 * 1024 * 1024
         ),
         name="exchange",
     )(series, modes.reshape(1, -1), query_weight, mix_weight, out_weight)
@@ -469,14 +467,14 @@
         inverse_kernel,
         out_shape=jax.ShapeDtypeStruct((series_count, steps, group), BF16),
         in_specs=[any_space, any_space],
-        out_specs=any_space,
+        out_specs=hbm,
         scratch_shapes=[
             vm((PARTS, steps, 256), BF16),
-            vm((PARTS, 2, 3, 256, group), BF16),
+            vm((PARTS, RING, 2, RING, 3, 16, group), BF16),
             vm((series_count, steps, group), BF16),
             dma((PARTS,)), dma((PARTS,)), dma((series_count,)),
         ],
-        compiler_params=pltpu.CompilerParams(vmem_limit_bytes=60 * 1024 * 1024),
+        compiler_params=pltpu.CompilerParams(vmem_limit_bytes=40 * 1024 * 1024),
         name="inverse",
     )(tables, gathered)
 

time: 55.3 us -> 58.9 us (1.065)
  local copies, waits for them, and re-layouts: 0 us -> 5.16 us
  Pallas kernels: 55.2 us -> 53.4 us
    unnamed x0 -> x10, local copies, waits for them, and re-layouts: none -> 5.16 us
    pallas_call x1, Pallas kernels: 6.24 us -> 5.21 us  [body(): pl.pallas_call(inverse_kernel, out_shape=jax.ShapeDtypeStruct((series_cou...]
    pallas_call x1, Pallas kernels: 48.9 us -> 48.2 us  [body(): pl.pallas_call(functools.partial(exchange_kernel, scale), out_shape=(jax....]
where the time goes in v5:
time: 58.9 us; the launch traced here: 58.6 us
  Pallas kernels  53.4 us (91%)
  local copies, waits for them, and re-layouts  5.16 us (9%)
    pallas_call x1, Pallas kernels, body(): pl.pallas_call(functools.partial(exchange_kernel, scale), out_shape=(jax....  48.2 us
    pallas_call x1, Pallas kernels, body(): pl.pallas_call(inverse_kernel, out_shape=jax.ShapeDtypeStruct((series_cou...  5.21 us
    unnamed x10, local copies, waits for them, and re-layouts  5.16 us

profile of v5, /device:TPU:0, one launch (start us, length us, event | category | flops | bytes accessed | tf_op | source)
XLA Modules:
  0.0 58.6 jit_solution(16324578163103232754)
XLA Ops:
  0.0 0.0 copy-start.1
  0.0 0.9 %copy-done.1 = bf16[512,256]{1,0:T(8,128)(2,1)S(1)} copy-done((bf16[512,256]{1,0:T(8,128)(2,1)S(1)}, bf16[512,256]{1,0:T(8,128)(2,1)}, u32[]{:S(2)}) %copy-start.1) | copy-done | bytes 262168
  1.0 0.0 copy-start.2
  1.0 0.9 %copy-done.2 = f32[2,4,64,128]{3,2,1,0:T(8,128)S(1)} copy-done((f32[2,4,64,128]{3,2,1,0:T(8,128)S(1)}, f32[2,4,64,128]{3,2,1,0:T(8,128)}, u32[]{:S(2)}) %copy-start.2) | copy-done | bytes 262168
  1.9 0.0 copy-start.3
  1.9 0.9 %copy-done.3 = bf16[512,256]{1,0:T(8,128)(2,1)S(1)} copy-done((bf16[512,256]{1,0:T(8,128)(2,1)S(1)}, bf16[512,256]{1,0:T(8,128)(2,1)}, u32[]{:S(2)}) %copy-start.3) | copy-done | bytes 262168
  2.9 0.0 copy-start.4
  2.9 0.7 %copy-done.4 = s32[128]{0:T(128)S(1)} copy-done((s32[128]{0:T(128)S(1)}, s32[128]{0:T(128)}, u32[]{:S(2)}) %copy-start.4) | copy-done | bytes 536
  3.5 48.2 %exchange.1 = (bf16[3,1024,256]{2,1,0:T(8,128)(2,1)S(1)}, bf16[3,4,2,4,3,16,256]{6,5,4,3,2,1,0:T(8,128)(2,1)}) custom-call(bf16[16,1024,512]{2,1,0:T(8,128)(2,1)} %series.1, s32[1,128]{1,0:T(1,128)S(1)} %bitcast.1, bf16[512,256]{1,0:T(8,128)(2,1)S(1)} %copy-done.1, f32[2,4,64,128]{3,2,1,0:T(8,128)S(1)} %copy-done.2, bf16[512,256]{1,0:T(8,128)(2,1)S(1)} %copy-done.3), custom_call_target="tpu_custom_call" | custom-call | tf_op jit(solution)/shard_map/exchange/pallas_call | solution.py:425
  51.8 0.0 copy-start
  51.8 1.7 %copy-done = bf16[3,4,2,4,3,16,256]{6,5,4,3,2,1,0:T(8,128)(2,1)S(1)} copy-done((bf16[3,4,2,4,3,16,256]{6,5,4,3,2,1,0:T(8,128)(2,1)S(1)}, bf16[3,4,2,4,3,16,256]{6,5,4,3,2,1,0:T(8,128)(2,1)}, u32[]{:S(2)}) %copy-start) | copy-done | bytes 2359320
  53.4 5.2 %inverse.1 = bf16[16,1024,256]{2,1,0:T(8,128)(2,1)} custom-call(bf16[3,1024,256]{2,1,0:T(8,128)(2,1)S(1)} %get-tuple-element.7.tab_in, bf16[3,4,2,4,3,16,256]{6,5,4,3,2,1,0:T(8,128)(2,1)S(1)} %copy-done), custom_call_target="tpu_custom_call" | custom-call | tf_op jit(solution)/shard_map/inverse/pallas_call | solution.py:466
Async XLA Ops:
  0.0 0.9 %copy-start.1 = (bf16[512,256]{1,0:T(8,128)(2,1)S(1)}, bf16[512,256]{1,0:T(8,128)(2,1)}, u32[]{:S(2)}) copy-start(bf16[512,256]{1,0:T(8,128)(2,1)} %wq_in.1) | copy-start | bytes 786436
  1.0 0.9 %copy-start.2 = (f32[2,4,64,128]{3,2,1,0:T(8,128)S(1)}, f32[2,4,64,128]{3,2,1,0:T(8,128)}, u32[]{:S(2)}) copy-start(f32[2,4,64,128]{3,2,1,0:T(8,128)} %mix_in.1) | copy-start | bytes 786436
  1.9 0.9 %copy-start.3 = (bf16[512,256]{1,0:T(8,128)(2,1)S(1)}, bf16[512,256]{1,0:T(8,128)(2,1)}, u32[]{:S(2)}) copy-start(bf16[512,256]{1,0:T(8,128)(2,1)} %wo_in.1) | copy-start | bytes 786436
  2.9 0.7 %copy-start.4 = (s32[128]{0:T(128)S(1)}, s32[128]{0:T(128)}, u32[]{:S(2)}) copy-start(s32[128]{0:T(128)} %param.6) | copy-start | bytes 1540
  51.8 1.7 %copy-start = (bf16[3,4,2,4,3,16,256]{6,5,4,3,2,1,0:T(8,128)(2,1)S(1)}, bf16[3,4,2,4,3,16,256]{6,5,4,3,2,1,0:T(8,128)(2,1)}, u32[]{:S(2)}) copy-start(bf16[3,4,2,4,3,16,256]{6,5,4,3,2,1,0:T(8,128)(2,1)} %get-tuple-element.8.gat_in) | copy-start | bytes 7077892
